TPU v7x, 32 devices: a whole 2x2x4 slice. The times are simulated.
32 devices in a mesh: patch: 2 (over y), sky: 4 (over z), exp: 2 (over core), band: 2 (over x).
Axes of the slice: x: 2, y: 2, z: 4, core: 2. Of those that a mesh axis runs over, the one named last changes fastest.
Arguments:
- images: bfloat16 [2, 20, 1024, 512], P('band', 'exp', ('patch', 'sky')), parts along dimension 2, may hold values from -400 to 400
- valid_mask: int32 [2, 20, 1024, 512], P('band', 'exp', ('patch', 'sky')), parts along dimension 2, may hold values from 0 to 1, as said below
- row_kernel: float32 [2, 20, 31], P('band', 'exp'), may hold values from 0.01 to 0.06
- col_kernel: float32 [2, 20, 31], P('band', 'exp'), may hold values from 0.01 to 0.06
- exp_group: int32 [2, 20], P('band', 'exp'), may hold values from 0 to 15
- zero_point: float32 [2, 16], P('band'), may hold values from 0.5 to 2
- psf_row: float32 [2, 31], P('band'), may hold values from 0.01 to 0.06
- psf_col: float32 [2, 31], P('band'), may hold values from 0.01 to 0.06
Outputs:
- coadd_image: float32 [2, 1024, 512], P('band', ('patch', 'sky')), parts along dimension 1
- detection: float32 [1024, 512], P(('patch', 'sky'), 'band'), parts along dimension 0
There are 2 independent parts, one for each index of `patch`. A program takes and returns all parts, laid end to end along the dimension named above; an argument that names none is the same for every part. Nothing has to cross between parts.
Inputs may be any that keep to these rules, and one draw needn't show every extreme that they name: For every band and pixel at least 10 of the 20 visits have valid_mask 1; exactly that many at some pixels, all of them at others.
All inputs are finite; a program needn't handle non-finite values.
Results may differ from a plain program's by a relative error of at most 0.0006.
Values may be sent and summed in bfloat16 or wider, within the bound.
A program may use at most 64 MiB of HBM per device.

v0:
```python
import jax
import jax.numpy as jnp
from jax import lax
from jax.sharding import PartitionSpec as P

HALF = 15
REJECT = 4
GROUPS = 16
TAPS = 31


SENTINEL = 1e30
EPSILON = 1e-05


def padded_2(value, sides, width):
    for axis, dim in sides:
        size, length = (lax.axis_size(axis), value.shape[dim])
        up = [(i, (i + 1) % size) for i in range(size - 1)]
        down = [(j, i) for i, j in up]
        last = lax.slice_in_dim(value, length - width, length, axis=dim)
        first = lax.slice_in_dim(value, 0, width, axis=dim)
        before = lax.ppermute(last, axis, up)
        after = lax.ppermute(first, axis, down)
        value = jnp.concatenate([before, value, after], axis=dim)
    return value


def merged_2(part, axis, combine):
    gathered = jax.tree.map(lambda a: lax.all_gather(a, axis), part)

    def take(source):
        return jax.tree.map(lambda a: lax.dynamic_index_in_dim(a, source, 0, False), gathered)

    return lax.fori_loop(
        1, lax.axis_size(axis), lambda source, state: combine(state, take(source)), take(0)
    )


def shortened(value):
    return jax.tree.map(lambda a: a.astype(jnp.bfloat16) if a.dtype == jnp.float32 else a, value)


def rows_filter(padded, kernel, height):
    result = kernel[..., 0][..., None, None] * padded[..., 0:height, :]
    for offset in range(1, TAPS):
        result = (
            result + kernel[..., offset][..., None, None] * padded[..., offset : offset + height, :]
        )
    return result


def cols_filter(grid_in, kernel):
    columns = grid_in.shape[-1]
    widths = [(0, 0)] * (grid_in.ndim - 1) + [(HALF, HALF)]
    padded = jnp.pad(grid_in, widths)
    result = kernel[..., 0][..., None, None] * padded[..., 0:columns]
    for offset in range(1, TAPS):
        result = (
            result + kernel[..., offset][..., None, None] * padded[..., offset : offset + columns]
        )
    return result


def insert_high(sorted_list, incoming):
    updated = []
    for position in range(REJECT):
        updated.append(jnp.maximum(sorted_list[position], incoming))
        incoming = jnp.minimum(sorted_list[position], incoming)
    return tuple(updated)


def insert_low(sorted_list, incoming):
    updated = []
    for position in range(REJECT):
        updated.append(jnp.minimum(sorted_list[position], incoming))
        incoming = jnp.maximum(sorted_list[position], incoming)
    return tuple(updated)


def visit_stats(visit_values, usable):
    plane = visit_values.shape[1:]
    upper_list = tuple((jnp.full(plane, -SENTINEL, jnp.float32) for position in range(REJECT)))
    lower_list = tuple((jnp.full(plane, SENTINEL, jnp.float32) for position in range(REJECT)))
    for visit_num in range(visit_values.shape[0]):
        current = visit_values[visit_num]
        is_live = usable[visit_num]
        upper_list = insert_high(upper_list, jnp.where(is_live, current, -SENTINEL))
        lower_list = insert_low(lower_list, jnp.where(is_live, current, SENTINEL))
    flux_sum = jnp.sum(jnp.where(usable, visit_values, jnp.float32(0.0)), axis=0)
    valid_count = jnp.sum(usable.astype(jnp.float32), axis=0)
    return (jnp.stack(upper_list), jnp.stack(lower_list), flux_sum, valid_count)


def combine_lists(left_side, right_side):
    upper_list = tuple((left_side[0][position] for position in range(REJECT)))
    lower_list = tuple((left_side[1][position] for position in range(REJECT)))
    for position in range(REJECT):
        upper_list = insert_high(upper_list, right_side[0][position])
        lower_list = insert_low(lower_list, right_side[1][position])
    return (
        jnp.stack(upper_list),
        jnp.stack(lower_list),
        left_side[2] + right_side[2],
        left_side[3] + right_side[3],
    )


def coadd_from(summary):
    upper_sum = jnp.sum(summary[0], axis=0)
    lower_sum = jnp.sum(summary[1], axis=0)
    return (summary[2] - upper_sum - lower_sum) / (summary[3] - 2 * REJECT)


def on_device(images, valid_mask, row_kernel, col_kernel, exp_group, zero_point, psf_row, psf_col):
    height = images.shape[2]
    padded = padded_2(images[0], (("sky", 1),), HALF)
    matches = exp_group[0][:, None] == jnp.arange(GROUPS, dtype=jnp.int32)[None, :]
    flux_scale = jnp.sum(jnp.where(matches, zero_point[0][None, :], jnp.float32(0.0)), axis=1)
    smeared = cols_filter(
        rows_filter(padded.astype(jnp.float32), row_kernel[0], height), col_kernel[0]
    )
    scaled_visits = flux_scale[:, None, None] * smeared
    usable = valid_mask[0] == 1
    summary = visit_stats(scaled_visits, usable)
    merged = merged_2(summary, "exp", combine_lists)
    coadd_image = coadd_from(merged)
    coadd_pad = padded_2(shortened(coadd_image), (("sky", 0),), HALF).astype(coadd_image.dtype)
    filtered = cols_filter(rows_filter(coadd_pad, psf_row[0], height), psf_col[0])
    energy = filtered * filtered
    energy_sum = lax.psum(jnp.sum(energy), "sky")
    variance = energy_sum / (height * lax.axis_size("sky") * energy.shape[1]) + EPSILON
    detection = lax.psum_scatter(energy / variance, "band", scatter_dimension=1, tiled=True)
    return (coadd_image[None], detection)


def solution(mesh):
    placed = (
        P("band", "exp", ("patch", "sky"), None),
        P("band", "exp", ("patch", "sky"), None),
        P("band", "exp", None),
        P("band", "exp", None),
        P("band", "exp"),
        P("band", None),
        P("band", None),
        P("band", None),
    )
    return jax.shard_map(
        on_device,
        mesh=mesh,
        in_specs=placed,
        out_specs=(P("band", ("patch", "sky"), None), P(("patch", "sky"), "band")),
        check_vma=False,
    )
```

profile of v0, /device:TPU:0, one launch (start us, length us, event | category | flops | bytes accessed | tf_op | source)
XLA Modules:
  0.0 164.7 jit_solution(17825145032995338779)
XLA Ops:
  7.2 1.0 fusion.270
  8.3 5.0 %collective-permute-start = (bf16[10,15,512]{2,1,0:T(8,128)(2,1)S(1)}, bf16[10,15,512]{2,1,0:T(8,128)(2,1)S(1)}, u32[]{:S(2)}, u32[]{:S(2)}) collective-permute-start(bf16[10,15,512]{2,1,0:T(8,128)(2,1)S(1)} %get-tuple-element.137), channel_id=1, source_target_pairs={{0,4},{4,8},{8,12},{1,5},{5,9},{9,13},{2,6},{6,10},{10,14},{3,7},{... | collective-permute-start | bytes 460808 | tf_op jit(solution)/shard_map/ppermute | solution.py:23
  13.2 1.3 collective-permute-start.1
  14.5 0.7 copy.14
  16.1 0.7 copy.15
  16.8 0.9 select_reduce_fusion.1
  18.5 2.3 %collective-permute-done.1 = bf16[10,15,512]{2,1,0:T(8,128)(2,1)S(1)} collective-permute-done((bf16[10,15,512]{2,1,0:T(8,128)(2,1)S(1)}, bf16[10,15,512]{2,1,0:T(8,128)(2,1)S(1)}, u32[]{:S(2)}, u32[]{:S(2)}) %collective-permute-start.1) | collective-permute-done | bytes 153632 | tf_op jit(solution)/shard_map/ppermute | solution.py:24
  20.8 1.8 %maximum_convert_fusion = f32[10,158,512]{2,1,0:T(8,128)S(1)} fusion(bf16[10,15,512]{2,1,0:T(8,128)(2,1)S(1)} %collective-permute-done.1, bf16[10,128,512]{2,1,0:T(8,128)(2,1)} %bitcast.349, bf16[10,15,512]{2,1,0:T(8,128)(2,1)S(1)} %collective-permute-done), kind=kLoop, calls=%fused_computation.154 | loop fusion | flops 4853760 | bytes 4853760 | tf_op jit(solution)/shard_map/convert_element_type | solution.py:121
  22.6 10.6 %fusion.61 = f32[10,128,512]{2,1,0:T(8,128)S(1)} fusion(f32[10,158,512]{2,1,0:T(8,128)S(1)} %maximum_convert_fusion, f32[10]{0:T(128)S(1)} %get-tuple-element.66, f32[10]{0:T(128)S(1)} %get-tuple-element.67, f32[10]{0:T(128)S(1)} %get-tuple-element.68, f32[10]{0:T(128)S(1)} %get-tuple-element.69, f32[10]{0:T(128)S(1)} %get-tuple-element.70, ...), kind=kLoop, calls=%fused_computation.92 | loop fusion | flops 39976960 | bytes 83887320 | tf_op jit(solution)/shard_map/add | solution.py:48
  33.2 21.9 %convert_reduce_fusion = (f32[128,512]{1,0:T(8,128)S(1)}, f32[128,512]{1,0:T(8,128)}, pred[1,10,128,512]{3,2,1,0:T(8,128)(4,1)S(1)}, f32[10,128,512]{2,1,0:T(8,128)S(1)}) fusion(s32[1,10,128,512]{3,2,1,0:T(8,128)S(1)} %copy-done, f32[10]{0:T(128)S(1)} %get-tuple-element.25, f32[10]{0:T(128)S(1)} %get-tuple-element.26, f32[10]{0:T(128)S(1)} %get-tuple-element.27, ...), kind=kLoop, calls=%fused_computation.152 | loop fusion | flops 43778048 | bytes 9045248 | tf_op jit(solution)/shard_map/reduce_sum | solution.py:91
  55.5 0.6 minimum_minimum_fusion.1
  56.5 1.1 pad_maximum_fusion.1
  58.1 0.6 maximum_maximum_fusion.1
  59.2 1.1 pad_maximum_fusion
  60.3 0.7 fusion.275
  61.0 0.7 fusion.274
  61.8 0.7 fusion.272
  62.5 2.4 %all-gather = f32[256,512]{1,0:T(8,128)S(1)} all-gather(f32[128,512]{1,0:T(8,128)S(1)} %copy-done.1), channel_id=2, replica_groups=mesh['patch'=2,'sky'=4,'exp'=2,'band'=2] {'exp'}, dimensions={0}, use_global_device_ids=true | all-gather | bytes 786432 | tf_op jit(solution)/shard_map/all_gather | solution.py:30
  64.9 2.2 %all-gather.3 = f32[256,512]{1,0:T(8,128)S(1)} all-gather(f32[128,512]{1,0:T(8,128)S(1)} %get-tuple-element.22), channel_id=5, replica_groups=mesh['patch'=2,'sky'=4,'exp'=2,'band'=2] {'exp'}, dimensions={0}, use_global_device_ids=true | all-gather | bytes 786432 | tf_op jit(solution)/shard_map/all_gather | solution.py:30
  67.1 1.5 all-gather.9.cloned.1.call-done
  68.6 13.3 %all-gather.7.cloned.1.call-done = f32[8,128,512]{2,1,0:T(8,128)} async-done(((f32[4,128,512]{2,1,0:T(8,128)}), f32[8,128,512]{2,1,0:T(8,128)}) %all-gather.7.cloned.1.call-update) | async-done | bytes 2097168 | tf_op jit(solution)/shard_map/all_gather | solution.py:30
  81.9 2.8 %fusion.206 = (bf16[128,512]{1,0:T(8,128)(2,1)S(1)}, f32[1,1,128,512]{3,2,1,0:T(8,128)S(1)}, f32[1,1,128,512]{3,2,1,0:T(8,128)S(1)}) fusion(f32[256,512]{1,0:T(8,128)S(1)} %all-gather, f32[256,512]{1,0:T(8,128)S(1)} %all-gather.3, f32[2,4,128,512]{3,2,1,0:T(8,128)} %bitcast.347, f32[2,4,128,512]{3,2,1,0:T(8,128)} %bitcast.346), kind=kLoop, calls=%fused_computation.343 | loop fusion | flops 4521984 | bytes 5898240 | tf_op jit(solution)/shard_map/convert_element_type | solution.py:41
  84.7 3.7 %collective-permute-start.2 = (bf16[15,512]{1,0:T(8,128)(2,1)S(1)}, bf16[15,512]{1,0:T(8,128)(2,1)S(1)}, u32[]{:S(2)}, u32[]{:S(2)}) collective-permute-start(bf16[15,512]{1,0:T(8,128)(2,1)S(1)} %get-tuple-element.139), channel_id=1, source_target_pairs={{0,4},{4,8},{8,12},{1,5},{5,9},{9,13},{2,6},{6,10},{10,14},{3,7},{... | collective-permute-start | bytes 46088 | tf_op jit(solution)/shard_map/ppermute | solution.py:23
  88.4 1.3 collective-permute-start.3
  89.7 0.7 fusion.273
  90.4 3.6 %collective-permute-done.3 = bf16[15,512]{1,0:T(8,128)(2,1)S(1)} collective-permute-done((bf16[15,512]{1,0:T(8,128)(2,1)S(1)}, bf16[15,512]{1,0:T(8,128)(2,1)S(1)}, u32[]{:S(2)}, u32[]{:S(2)}) %collective-permute-start.3) | collective-permute-done | bytes 15392 | tf_op jit(solution)/shard_map/ppermute | solution.py:24
  94.1 20.1 %fusion.166 = f32[128,512]{1,0:T(8,128)S(1)} fusion(f32[158,512]{1,0:T(8,128)S(1)} %maximum_convert_fusion.1, f32[]{:T(128)} %bitcast.53, f32[]{:T(128)} %bitcast.52, f32[]{:T(128)} %bitcast.51, f32[]{:T(128)} %bitcast.50, f32[]{:T(128)} %bitcast.49, f32[]{:T(128)} %bitcast.48, f32[]{:T(128)} %bitcast.47, f32[]{:T(128)} %bitcast.46, f32[]{:T(128)} %bitcast.45, ...), kind=kLoop, calls=%fused_computation.268 | loop fusion | flops 3997696 | bytes 8388732 | tf_op jit(solution)/shard_map/add | solution.py:48
  114.2 22.0 %fusion.241 = (f32[]{:T(128)}, f32[128,512]{1,0:T(8,128)S(1)}) fusion(f32[]{:T(128)} %bitcast.83, f32[]{:T(128)} %bitcast.82, f32[]{:T(128)} %bitcast.81, f32[]{:T(128)} %bitcast.80, f32[]{:T(128)} %bitcast.79, f32[]{:T(128)} %bitcast.78, f32[]{:T(128)} %bitcast.77, f32[]{:T(128)} %bitcast.76, f32[]{:T(128)} %bitcast.75, f32[]{:T(128)} %bitcast.74, ...), kind=kLoop, calls=%fused_computation.490 | loop fusion | flops 4128767 | bytes 524416 | tf_op jit(solution)/shard_map/reduce_sum | solution.py:131
  136.2 10.5 %psum.7 = f32[]{:T(128)} all-reduce(f32[]{:T(128)} %get-tuple-element.96), channel_id=1, replica_groups=mesh['patch'=2,'sky'=4,'exp'=2,'band'=2] {'sky'}, use_global_device_ids=true, to_apply=%region_4.5 | all-reduce | flops 1 | bytes 8 | tf_op jit(solution)/shard_map/psum | solution.py:131
  147.4 0.7 broadcast_divide_fusion
  148.1 0.9 bitcast_divide_fusion
  149.0 9.2 %reduce-scatter.2.cloned.1.call-done = f32[128,256]{1,0:T(8,128)} async-done(((f32[128,512]{1,0:T(8,128)}), f32[128,256]{1,0:T(8,128)}) %reduce-scatter.2.cloned.1.call-update) | async-done | bytes 131088 | tf_op jit(solution)/shard_map/reduce_scatter | solution.py:133
  (26 shorter events, 3.7 us)
Async XLA Ops:
  7.2 61.4 %all-gather.9.cloned.1.call-start = ((), (), s32[]{:S(2)}) async-start(), calls=%async_computation.3 | async-start | bytes 3145728 | tf_op jit(solution)/shard_map/all_gather | solution.py:30
  8.3 10.2 %collective-permute-start = (bf16[10,15,512]{2,1,0:T(8,128)(2,1)S(1)}, bf16[10,15,512]{2,1,0:T(8,128)(2,1)S(1)}, u32[]{:S(2)}, u32[]{:S(2)}) collective-permute-start(bf16[10,15,512]{2,1,0:T(8,128)(2,1)S(1)} %get-tuple-element.137), channel_id=1, source_target_pairs={{0,4},{4,8},{8,12},{1,5},{5,9},{9,13},{2,6},{6,10},{10,14},{3,7},{... | collective-permute-start | bytes 460808 | tf_op jit(solution)/shard_map/ppermute | solution.py:23
  13.2 7.6 %collective-permute-start.1 = (bf16[10,15,512]{2,1,0:T(8,128)(2,1)S(1)}, bf16[10,15,512]{2,1,0:T(8,128)(2,1)S(1)}, u32[]{:S(2)}, u32[]{:S(2)}) collective-permute-start(bf16[10,15,512]{2,1,0:T(8,128)(2,1)S(1)} %get-tuple-element.138), channel_id=1, source_target_pairs={{4,0},{8,4},{12,8},{5,1},{9,5},{13,9},{6,2},{10,6},{14,10},{7,3},{... | collective-permute-start | bytes 460808 | tf_op jit(solution)/shard_map/ppermute | solution.py:24
  22.6 10.6 %copy-start = (s32[1,10,128,512]{3,2,1,0:T(8,128)S(1)}, s32[1,10,128,512]{3,2,1,0:T(8,128)}, u32[]{:S(2)}) copy-start(s32[1,10,128,512]{3,2,1,0:T(8,128)} %param.9) | copy-start | bytes 7864324
  57.6 24.3 %all-gather.7.cloned.1.call-start = ((), (), s32[]{:S(2)}) async-start(), calls=%async_computation.2 | async-start | bytes 3145728 | tf_op jit(solution)/shard_map/all_gather | solution.py:30
  58.7 1.7 %copy-start.2 = (f32[1,31]{1,0:T(1,128)S(1)}, f32[1,31]{1,0:T(1,128)}, u32[]{:S(2)}) copy-start(f32[1,31]{1,0:T(1,128)} %param.14) | copy-start | bytes 376
  58.7 3.1 %copy-start.3 = (f32[1,31]{1,0:T(1,128)S(1)}, f32[1,31]{1,0:T(1,128)}, u32[]{:S(2)}) copy-start(f32[1,31]{1,0:T(1,128)} %param.15) | copy-start | bytes 376
  59.1 3.4 %copy-start.1 = (f32[128,512]{1,0:T(8,128)S(1)}, f32[128,512]{1,0:T(8,128)}, u32[]{:S(2)}) copy-start(f32[128,512]{1,0:T(8,128)} %get-tuple-element.23) | copy-start | bytes 786436
  60.3 97.9 %reduce-scatter.2.cloned.1.call-start = ((), (), s32[]{:S(2)}) async-start(), calls=%async_computation.1 | async-start | bytes 393216 | tf_op jit(solution)/shard_map/reduce_scatter | solution.py:133
  84.7 5.7 %collective-permute-start.2 = (bf16[15,512]{1,0:T(8,128)(2,1)S(1)}, bf16[15,512]{1,0:T(8,128)(2,1)S(1)}, u32[]{:S(2)}, u32[]{:S(2)}) collective-permute-start(bf16[15,512]{1,0:T(8,128)(2,1)S(1)} %get-tuple-element.139), channel_id=1, source_target_pairs={{0,4},{4,8},{8,12},{1,5},{5,9},{9,13},{2,6},{6,10},{10,14},{3,7},{... | collective-permute-start | bytes 46088 | tf_op jit(solution)/shard_map/ppermute | solution.py:23
  88.4 5.6 %collective-permute-start.3 = (bf16[15,512]{1,0:T(8,128)(2,1)S(1)}, bf16[15,512]{1,0:T(8,128)(2,1)S(1)}, u32[]{:S(2)}, u32[]{:S(2)}) collective-permute-start(bf16[15,512]{1,0:T(8,128)(2,1)S(1)} %get-tuple-element.140), channel_id=1, source_target_pairs={{4,0},{8,4},{12,8},{5,1},{9,5},{13,9},{6,2},{10,6},{14,10},{7,3},{... | collective-permute-start | bytes 46088 | tf_op jit(solution)/shard_map/ppermute | solution.py:24
Sparse Core Ops, SparseCore 0:
  57.7 10.7 all-gather.8
  70.1 11.7 all-gather.6
  148.2 9.8 reduce-scatter.1
where the time goes:
time: 166 us; the launch traced here: 165 us
  other arithmetic  86.7 us (52%)
  waiting for transfers between devices  30 us (18%)
  blocking collectives  15.1 us (9%)
  between operations  14.6 us (9%)
  starting transfers between devices  11.3 us (7%)
  local copies, waits for them, and re-layouts  7.06 us (4%)
    add x2, other arithmetic, rows_filter(): result + kernel[..., offset][..., None, None] * padded[..., offset:offset...  30.7 us
    reduce_sum x1, other arithmetic, on_device(): energy_sum = lax.psum(jnp.sum(energy), 'sky')  22 us
    reduce_sum x1, other arithmetic, visit_stats(): valid_count = jnp.sum(usable.astype(jnp.float32), axis=0)  21.9 us
    all_gather x2, waiting for transfers between devices, merged_2(): gathered = jax.tree.map(lambda a: lax.all_gather(a, axis), part)  14.8 us
    psum x1, blocking collectives, on_device(): energy_sum = lax.psum(jnp.sum(energy), 'sky')  10.5 us
    reduce_scatter x1, waiting for transfers between devices, on_device(): lax.psum_scatter(energy / variance, 'band', scatter_dimension=1, tiled=True)  9.2 us
    ppermute x2, starting transfers between devices, padded_2(): before = lax.ppermute(last, axis, up)  8.62 us
    ppermute x2, waiting for transfers between devices, padded_2(): after = lax.ppermute(first, axis, down)  5.89 us
  transfers between devices with their start and end apart: 7, of which 5 were waited for; matrix products, arithmetic and copies ran while one was open for 6% of the time, Pallas kernels for 0%

commit v1 on v0

v1 whole, which is shorter than its diff:
```python
import functools

import jax
import jax.numpy as jnp
from jax import lax
from jax.experimental import pallas as pl
from jax.experimental.pallas import tpu as pltpu
from jax.sharding import PartitionSpec as P

MESH = pl.DeviceIdType.MESH
HALF = 15
REJECT = 4
TAPS = 31
SENTINEL = 1e30
EPSILON = 1e-05
PAD = 16
TILE = 128
CHUNKS = 4
BF = jnp.bfloat16
F32 = jnp.float32


def parts(value):
    high = value.astype(BF)
    return high, (value - high.astype(F32)).astype(BF)


def mm(a, b):
    return jnp.dot(a, b, preferred_element_type=F32)


def cols_filter(high, low, wh_ref, wl_ref):
    columns = high.shape[1]
    outs = []
    for start in range(0, columns, 2 * TILE):
        lo_in, hi_in = max(start - TILE, 0), min(start + 3 * TILE, columns)
        base = lo_in - (start - TILE)
        span = pl.ds(base, hi_in - lo_in)
        wh, wl = wh_ref[span, :], wl_ref[span, :]
        h, l = high[:, lo_in:hi_in], low[:, lo_in:hi_in]
        outs.append(mm(h, wh) + mm(l, wh) + mm(h, wl))
    return outs


def insert(ordered, incoming, first, second):
    updated = []
    for held in ordered:
        updated.append(first(held, incoming))
        incoming = second(held, incoming)
    if len(updated) < REJECT:
        updated.append(incoming)
    return updated


def kernel(
    n_sky, n_band,
    img, mask, rk, ck, pr, pc, eg, zp,
    coadd_out, det_out,
    x, msk, taps_r, taps_c, trow, wh, wl, vals, lists, other, cpad, energy, peer_energy, sums, det,
    img_sem, mask_sem, halo_send, halo_recv, list_send, list_recv, co_send, co_recv, sum_send, sum_recv,
    en_send, en_recv, out_sem,
):
    visits, height, columns = img.shape[1:]
    width = columns // n_band
    crows = height // CHUNKS
    sky, band, exp = lax.axis_index("sky"), lax.axis_index("band"), lax.axis_index("exp")
    has_before, has_after = sky > 0, sky < n_sky - 1
    n_peer = n_sky * n_band
    me = sky * n_band + band

    load_img = pltpu.make_async_copy(img.at[0], x.at[:, pl.ds(PAD, height), :], img_sem)
    load_img.start()
    load_mask = pltpu.make_async_copy(mask.at[0], msk, mask_sem)
    load_mask.start()

    def peer_of(step):
        peer = lax.rem(me + step, n_peer)
        return {"sky": peer // n_band, "band": lax.rem(peer, n_band)}

    barrier = pltpu.get_barrier_semaphore()
    for step in range(1, n_peer):
        pl.semaphore_signal(barrier, inc=1, device_id=peer_of(step), device_id_type=MESH)
    pl.semaphore_signal(barrier, inc=1, device_id={"exp": 1 - exp}, device_id_type=MESH)

    taps_r[...] = jnp.zeros_like(taps_r)
    taps_c[...] = jnp.zeros_like(taps_c)
    taps_r[0:visits, 0:TAPS] = rk[0]
    taps_r[visits:visits + 1, 0:TAPS] = pr[...]
    for v in range(visits):
        taps_c[v:v + 1, 0:TAPS] = ck[0, v:v + 1] * zp[0, eg[0, v]]
    taps_c[visits:visits + 1, 0:TAPS] = pc[...]
    at_row = lax.broadcasted_iota(jnp.int32, (TILE, TILE), 0)
    at_col = lax.broadcasted_iota(jnp.int32, (TILE, TILE), 1)
    flip = (at_col == lax.rem(HALF - at_row + TILE, TILE)).astype(F32)
    taps_c[...] = jnp.dot(taps_c[...], flip, preferred_element_type=F32, precision=lax.Precision.HIGHEST)

    def build(v, carry):
        band_r = jnp.broadcast_to(taps_r[pl.ds(v, 1), :], (TILE, TILE))
        band_r = pltpu.roll(band_r, 1, 1, stride=1, stride_axis=0)
        high, low = parts(jnp.where(at_col >= at_row, band_r, 0.0))
        trow[v, 0:TILE, 0:TILE] = high
        trow[v, TILE:2 * TILE, 0:TILE] = low
        high, low = parts(jnp.where(at_col < at_row, band_r, 0.0))
        trow[v, 0:TILE, TILE:2 * TILE] = high
        trow[v, TILE:2 * TILE, TILE:2 * TILE] = low
        band_c = jnp.broadcast_to(taps_c[pl.ds(v, 1), :], (TILE, TILE))
        band_c = pltpu.roll(band_c, 0, 1, stride=1, stride_axis=0)
        before = at_row - at_col > TILE // 2
        after = at_col - at_row > TILE // 2
        zero = jnp.zeros((TILE, TILE), BF)
        for half, ref in enumerate((wh, wl)):
            b_prev = parts(jnp.where(before, band_c, 0.0))[half]
            b_next = parts(jnp.where(after, band_c, 0.0))[half]
            b_here = parts(jnp.where(before | after, 0.0, band_c))[half]
            for k, row in enumerate(((b_prev, zero), (b_here, b_prev), (b_next, b_here), (zero, b_next))):
                for n, block in enumerate(row):
                    ref[v, k * TILE:(k + 1) * TILE, n * TILE:(n + 1) * TILE] = block
        return carry

    lax.fori_loop(0, visits + 1, build, 0)
    pl.semaphore_wait(barrier, n_peer)

    def halo(v, side):
        start, land = ((height - PAD, 0), (0, PAD + height))[side]
        return pltpu.make_async_remote_copy(
            src_ref=img.at[0, v, pl.ds(start, PAD), :],
            dst_ref=x.at[v, pl.ds(land, PAD), :],
            send_sem=halo_send.at[side, v], recv_sem=halo_recv.at[side, v],
            device_id={"sky": lax.rem(sky + (1, n_sky - 1)[side], n_sky)}, device_id_type=MESH,
        )

    def start_halo(v, carry):
        @pl.when(has_after)
        def _():
            halo(v, 0).start()

        @pl.when(has_before)
        def _():
            halo(v, 1).start()
        return carry

    lax.fori_loop(0, visits, start_halo, 0)

    @pl.when(jnp.logical_not(has_before))
    def _():
        x[:, 0:PAD, :] = jnp.zeros((visits, PAD, columns), BF)
        cpad[0:PAD, :] = jnp.zeros((PAD, columns), F32)

    @pl.when(jnp.logical_not(has_after))
    def _():
        x[:, PAD + height:, :] = jnp.zeros((visits, PAD, columns), BF)
        cpad[PAD + height:, :] = jnp.zeros((PAD, columns), F32)

    load_img.wait()
    tall = height + 2 * PAD

    def convolve(v, carry):
        @pl.when(has_before)
        def _():
            halo(v, 0).wait_recv()

        @pl.when(has_after)
        def _():
            halo(v, 1).wait_recv()
        smeared = mm(trow[v, :, 0:tall], x[v])
        high, low = parts(smeared[0:height] + smeared[height:])
        for n, block in enumerate(cols_filter(high, low, wh.at[v], wl.at[v])):
            vals[v, :, n * 2 * TILE:(n + 1) * 2 * TILE] = block
        return carry

    lax.fori_loop(0, visits, convolve, 0)
    load_mask.wait()

    def exchange(c):
        return pltpu.make_async_remote_copy(
            src_ref=lists.at[c], dst_ref=other.at[c], send_sem=list_send.at[c], recv_sem=list_recv.at[c],
            device_id={"exp": 1 - exp}, device_id_type=MESH,
        )

    def select(c, carry):
        def group(g, inner):
            rows = pl.ds(pl.multiple_of(c * crows + g * 8, 8), 8)
            upper, lower, total, count = [], [], None, None
            for v in range(visits):
                value, used = vals[v, rows, :], msk[v, rows, :]
                live = used == 1
                upper = insert(upper, jnp.where(live, value, -SENTINEL), jnp.maximum, jnp.minimum)
                lower = insert(lower, jnp.where(live, value, SENTINEL), jnp.minimum, jnp.maximum)
                kept = jnp.where(live, value, 0.0)
                total = kept if total is None else total + kept
                count = used if count is None else count + used
            spot = pl.ds(pl.multiple_of(g * 8, 8), 8)
            for k, item in enumerate(upper + lower + [total, count.astype(F32)]):
                lists[c, k, spot, :] = item
            return inner

        lax.fori_loop(0, crows // 8, group, 0)
        exchange(c).start()
        return carry

    lax.fori_loop(0, CHUNKS, select, 0)

    def merge(c, carry):
        exchange(c).wait_recv()

        def group(g, inner):
            spot = pl.ds(pl.multiple_of(g * 8, 8), 8)
            own = [lists[c, k, spot, :] for k in range(2 * REJECT + 2)]
            far = [other[c, k, spot, :] for k in range(2 * REJECT + 2)]
            ends = [jnp.maximum(own[k], far[REJECT - 1 - k]) for k in range(REJECT)]
            ends += [jnp.minimum(own[REJECT + k], far[2 * REJECT - 1 - k]) for k in range(REJECT)]
            upper_sum = (ends[0] + ends[1]) + (ends[2] + ends[3])
            lower_sum = (ends[4] + ends[5]) + (ends[6] + ends[7])
            flux, count = own[8] + far[8], own[9] + far[9]
            rows = pl.ds(pl.multiple_of(PAD + c * crows + g * 8, 8), 8)
            cpad[rows, :] = (flux - upper_sum - lower_sum) / (count - 2 * REJECT)
            return inner

        lax.fori_loop(0, crows // 8, group, 0)
        return carry

    lax.fori_loop(0, CHUNKS, merge, 0)

    def co_halo(side):
        start, land = ((height, 0), (PAD, PAD + height))[side]
        return pltpu.make_async_remote_copy(
            src_ref=cpad.at[pl.ds(start, PAD), :], dst_ref=cpad.at[pl.ds(land, PAD), :],
            send_sem=co_send.at[side], recv_sem=co_recv.at[side],
            device_id={"sky": lax.rem(sky + (1, n_sky - 1)[side], n_sky)}, device_id_type=MESH,
        )

    store_coadd = pltpu.make_async_copy(cpad.at[pl.ds(PAD, height), :], coadd_out.at[0], out_sem.at[0])

    @pl.when(has_after)
    def _():
        co_halo(0).start()

    @pl.when(has_before)
    def _():
        co_halo(1).start()
    store_coadd.start()

    @pl.when(has_before)
    def _():
        co_halo(0).wait_recv()

    @pl.when(has_after)
    def _():
        co_halo(1).wait_recv()
    high, low = parts(cpad[...])
    both = mm(trow[visits, :, 0:tall], high)
    smeared = both[0:height] + both[height:] + mm(trow[visits, 0:height, 0:tall], low)
    high, low = parts(smeared)
    partial = jnp.zeros((8, TILE), F32)
    for n, block in enumerate(cols_filter(high, low, wh.at[visits], wl.at[visits])):
        squared = block * block
        energy[:, n * 2 * TILE:(n + 1) * 2 * TILE] = squared
        for r in range(0, height, 8):
            for q in range(0, 2 * TILE, TILE):
                partial = partial + squared[r:r + 8, q:q + TILE]
    sums[pl.ds(me, 1)] = partial[None]

    def send_sum(step):
        return pltpu.make_async_remote_copy(
            src_ref=sums.at[me], dst_ref=sums.at[me], send_sem=sum_send.at[step - 1], recv_sem=sum_recv.at[step - 1],
            device_id=peer_of(step), device_id_type=MESH,
        )

    def send_energy(step):
        target = lax.rem(band + step, n_band)
        return pltpu.make_async_remote_copy(
            src_ref=energy.at[:, pl.ds(pl.multiple_of(target * width, TILE), width)],
            dst_ref=peer_energy.at[step - 1],
            send_sem=en_send.at[step - 1], recv_sem=en_recv.at[step - 1],
            device_id={"band": target}, device_id_type=MESH,
        )

    for step in range(1, n_peer):
        send_sum(step).start()
    for step in range(1, n_band):
        send_energy(step).start()
    for step in range(1, n_peer):
        send_sum(step).wait_recv()

    pixels = height * n_sky * columns

    def inverse(source):
        total = sums[source]
        for s in range(1, n_sky):
            total = total + sums[source + s * n_band]
        return 1.0 / (jnp.sum(total, keepdims=True) / pixels + EPSILON)

    mine = pl.ds(pl.multiple_of(band * width, TILE), width)
    total = energy[:, mine] * inverse(band)
    for step in range(1, n_band):
        send_energy(step).wait_recv()
        total = total + peer_energy[step - 1] * inverse(lax.rem(band + n_band - step, n_band))
    det[...] = total
    store_det = pltpu.make_async_copy(det, det_out, out_sem.at[1])
    store_det.start()

    def drain(v, carry):
        @pl.when(has_after)
        def _():
            halo(v, 0).wait_send()

        @pl.when(has_before)
        def _():
            halo(v, 1).wait_send()
        return carry

    lax.fori_loop(0, visits, drain, 0)

    @pl.when(has_after)
    def _():
        co_halo(0).wait_send()

    @pl.when(has_before)
    def _():
        co_halo(1).wait_send()
    for c in range(CHUNKS):
        exchange(c).wait_send()
    for step in range(1, n_peer):
        send_sum(step).wait_send()
    for step in range(1, n_band):
        send_energy(step).wait_send()
    store_coadd.wait()
    store_det.wait()


def solution(mesh):
    n_sky, n_band = mesh.shape["sky"], mesh.shape["band"]

    def on_device(images, valid_mask, row_kernel, col_kernel, exp_group, zero_point, psf_row, psf_col):
        _, visits, height, columns = images.shape
        assert height == TILE and mesh.shape["exp"] == 2 and visits >= REJECT
        width = columns // n_band
        tall = height + 2 * PAD
        n_list = 2 * REJECT + 2
        crows = height // CHUNKS
        kernels = visits + 1
        table = -(-kernels // 8) * 8
        vmem, smem, hbm = (
            pl.BlockSpec(memory_space=space) for space in (pltpu.VMEM, pltpu.SMEM, pl.ANY)
        )
        dma = pltpu.SemaphoreType.DMA
        return pl.pallas_call(
            functools.partial(kernel, n_sky, n_band),
            out_shape=(
                jax.ShapeDtypeStruct((1, height, columns), F32),
                jax.ShapeDtypeStruct((height, width), F32),
            ),
            in_specs=[hbm, hbm, vmem, vmem, vmem, vmem, smem, smem],
            out_specs=(hbm, hbm),
            scratch_shapes=[
                pltpu.VMEM((visits, tall, columns), BF),
                pltpu.VMEM((visits, height, columns), jnp.int32),
                pltpu.VMEM((table, TILE), F32),
                pltpu.VMEM((table, TILE), F32),
                pltpu.VMEM((kernels, 2 * TILE, 2 * TILE), BF),
                pltpu.VMEM((kernels, 4 * TILE, 2 * TILE), BF),
                pltpu.VMEM((kernels, 4 * TILE, 2 * TILE), BF),
                pltpu.VMEM((visits, height, columns), F32),
                pltpu.VMEM((CHUNKS, n_list, crows, columns), F32),
                pltpu.VMEM((CHUNKS, n_list, crows, columns), F32),
                pltpu.VMEM((tall, columns), F32),
                pltpu.VMEM((height, columns), F32),
                pltpu.VMEM((n_band - 1, height, width), F32),
                pltpu.VMEM((n_sky * n_band, 8, TILE), F32),
                pltpu.VMEM((height, width), F32),
                dma, dma, dma((2, visits)), dma((2, visits)), dma((CHUNKS,)), dma((CHUNKS,)),
                dma((2,)), dma((2,)), dma((n_sky * n_band - 1,)), dma((n_sky * n_band - 1,)), dma((n_band - 1,)), dma((n_band - 1,)), dma((2,)),
            ],
            compiler_params=pltpu.CompilerParams(
                collective_id=0, has_side_effects=True, vmem_limit_bytes=48 * 1024 * 1024
            ),
        )(images, valid_mask, row_kernel, col_kernel, psf_row, psf_col, exp_group, zero_point)

    placed = (
        P("band", "exp", ("patch", "sky"), None),
        P("band", "exp", ("patch", "sky"), None),
        P("band", "exp", None),
        P("band", "exp", None),
        P("band", "exp"),
        P("band", None),
        P("band", None),
        P("band", None),
    )
    return jax.shard_map(
        on_device,
        mesh=mesh,
        in_specs=placed,
        out_specs=(P("band", ("patch", "sky"), None), P(("patch", "sky"), "band")),
        check_vma=False,
    )
```

time: 166 us -> 37.4 us (0.23)
  other arithmetic: 86.7 us -> 0 us
  waiting for transfers between devices: 30 us -> 0 us
  Pallas kernels: 0 us -> 28 us
  blocking collectives: 15.1 us -> 0 us
  between operations: 14.6 us -> 0.65 us
  starting transfers between devices: 11.3 us -> 0 us
    reduce_sum x3 -> x0, other arithmetic: 44.7 us -> none  [the longest x1 22 us: on_device(): energy_sum = lax.psum(jnp.sum(energy), 'sky')]
    add x2 -> x0, other arithmetic: 30.7 us -> none  [rows_filter(): result + kernel[..., offset][..., None, None] * padded[..., offset:offset...]
    pallas_call x0 -> x1, Pallas kernels: none -> 28 us  [on_device(): pl.pallas_call(functools.partial(kernel, n_sky, n_band), out_shape=(jax.S...]
    all_gather x2 -> x0, waiting for transfers between devices: 14.8 us -> none  [merged_2(): gathered = jax.tree.map(lambda a: lax.all_gather(a, axis), part)]
    ppermute x4 -> x0, starting transfers between devices: 11.2 us -> none  [the longest x2 8.62 us: padded_2(): before = lax.ppermute(last, axis, up)]
    psum x1 -> x0, blocking collectives: 10.5 us -> none  [on_device(): energy_sum = lax.psum(jnp.sum(energy), 'sky')]
    reduce_scatter x1 -> x0, waiting for transfers between devices: 9.2 us -> none  [on_device(): lax.psum_scatter(energy / variance, 'band', scatter_dimension=1, tiled=True)]
    unnamed x10 -> x16, local copies, waits for them, and re-layouts: 1.42 us -> 8.42 us
  transfers between devices with their start and end apart: 7 -> 0, of which waited for: 5 -> 0; matrix products, arithmetic and copies ran while one was open for 6% -> 0% of each run, Pallas kernels for 0% -> 0%
where the time goes in v1:
time: 37.4 us; the launch traced here: 37.1 us
  Pallas kernels  28 us (75%)
  local copies, waits for them, and re-layouts  8.42 us (23%)
  between operations  0.65 us (2%)
    pallas_call x1, Pallas kernels, on_device(): pl.pallas_call(functools.partial(kernel, n_sky, n_band), out_shape=(jax.S...  28 us
    unnamed x16, local copies, waits for them, and re-layouts  8.42 us

profile of v1, /device:TPU:0, one launch (start us, length us, event | category | flops | bytes accessed | tf_op | source)
XLA Modules:
  0.0 37.1 jit_solution(11626181739944879502)
XLA Ops:
  0.6 0.7 %copy.10.rk = f32[1,10,31]{2,1,0:T(8,128)S(1)} copy(f32[1,10,31]{2,0,1:T(1,128)} %param.10) | data formatting | bytes 2480 | tf_op args[2]
  1.3 0.7 %copy.11.ck = f32[1,10,31]{2,1,0:T(8,128)S(1)} copy(f32[1,10,31]{2,0,1:T(1,128)} %param.11) | data formatting | bytes 2480 | tf_op args[3]
  2.0 0.0 copy-start
  2.0 1.7 %copy-done = s32[1,10,128,512]{3,2,1,0:T(8,128)S(1)} copy-done((s32[1,10,128,512]{3,2,1,0:T(8,128)S(1)}, s32[1,10,128,512]{3,2,1,0:T(8,128)}, u32[]{:S(2)}) %copy-start) | copy-done | bytes 2621464
  3.8 0.0 copy-start.1
  3.8 1.3 %copy-done.1 = bf16[1,10,128,512]{3,2,1,0:T(8,128)(2,1)S(1)} copy-done((bf16[1,10,128,512]{3,2,1,0:T(8,128)(2,1)S(1)}, bf16[1,10,128,512]{3,2,1,0:T(8,128)(2,1)}, u32[]{:S(2)}) %copy-start.1) | copy-done | bytes 1310744
  5.1 0.0 copy-start.2
  5.1 0.7 %copy-done.2 = f32[1,31]{1,0:T(1,128)S(1)} copy-done((f32[1,31]{1,0:T(1,128)S(1)}, f32[1,31]{1,0:T(1,128)}, u32[]{:S(2)}) %copy-start.2) | copy-done | bytes 148
  5.7 0.0 copy-start.3
  5.7 0.7 %copy-done.3 = f32[1,31]{1,0:T(1,128)S(1)} copy-done((f32[1,31]{1,0:T(1,128)S(1)}, f32[1,31]{1,0:T(1,128)}, u32[]{:S(2)}) %copy-start.3) | copy-done | bytes 148
  6.4 0.0 copy-start.4
  6.4 0.7 %copy-done.4 = s32[1,10]{1,0:T(1,128)S(1)} copy-done((s32[1,10]{1,0:T(1,128)S(1)}, s32[1,10]{1,0:T(1,128)}, u32[]{:S(2)}) %copy-start.4) | copy-done | bytes 64
  7.0 0.0 copy-start.5
  7.0 0.7 %copy-done.5 = f32[1,16]{1,0:T(1,128)S(1)} copy-done((f32[1,16]{1,0:T(1,128)S(1)}, f32[1,16]{1,0:T(1,128)}, u32[]{:S(2)}) %copy-start.5) | copy-done | bytes 88
  7.7 28.0 %shard_map.95 = (f32[1,128,512]{2,1,0:T(8,128)S(1)}, f32[128,256]{1,0:T(8,128)S(1)}) custom-call(bf16[1,10,128,512]{3,2,1,0:T(8,128)(2,1)S(1)} %copy-done.1, s32[1,10,128,512]{3,2,1,0:T(8,128)S(1)} %copy-done, f32[1,10,31]{2,1,0:T(8,128)S(1)} %copy.10.rk, f32[1,10,31]{2,1,0:T(8,128)S(1)} %copy.11.ck, f32[1,31]{1,0:T(1,128)S(1)} %copy-done.2, ...), custom_call_target="tpu_custom_call" | custom-call | tf_op jit(solution)/shard_map/pallas_call | solution.py:347
  35.7 0.7 %copy.14 = f32[1,128,512]{2,1,0:T(8,128)} copy(f32[1,128,512]{2,1,0:T(8,128)S(1)} %get-tuple-element.4) | data formatting | bytes 524288
  36.4 0.7 %copy.15 = f32[128,256]{1,0:T(8,128)} copy(f32[128,256]{1,0:T(8,128)S(1)} %get-tuple-element.5) | data formatting | bytes 262144
Async XLA Ops:
  2.0 1.7 %copy-start = (s32[1,10,128,512]{3,2,1,0:T(8,128)S(1)}, s32[1,10,128,512]{3,2,1,0:T(8,128)}, u32[]{:S(2)}) copy-start(s32[1,10,128,512]{3,2,1,0:T(8,128)} %mask.1) | copy-start | bytes 7864324
  3.8 1.3 %copy-start.1 = (bf16[1,10,128,512]{3,2,1,0:T(8,128)(2,1)S(1)}, bf16[1,10,128,512]{3,2,1,0:T(8,128)(2,1)}, u32[]{:S(2)}) copy-start(bf16[1,10,128,512]{3,2,1,0:T(8,128)(2,1)} %img.1) | copy-start | bytes 3932164
  5.1 0.7 %copy-start.2 = (f32[1,31]{1,0:T(1,128)S(1)}, f32[1,31]{1,0:T(1,128)}, u32[]{:S(2)}) copy-start(f32[1,31]{1,0:T(1,128)} %pr.1) | copy-start | bytes 376
  5.7 0.7 %copy-start.3 = (f32[1,31]{1,0:T(1,128)S(1)}, f32[1,31]{1,0:T(1,128)}, u32[]{:S(2)}) copy-start(f32[1,31]{1,0:T(1,128)} %pc.1) | copy-start | bytes 376
  6.4 0.7 %copy-start.4 = (s32[1,10]{1,0:T(1,128)S(1)}, s32[1,10]{1,0:T(1,128)}, u32[]{:S(2)}) copy-start(s32[1,10]{1,0:T(1,128)} %eg.1) | copy-start | bytes 124
  7.0 0.7 %copy-start.5 = (f32[1,16]{1,0:T(1,128)S(1)}, f32[1,16]{1,0:T(1,128)}, u32[]{:S(2)}) copy-start(f32[1,16]{1,0:T(1,128)} %zp.1) | copy-start | bytes 196

commit v2 on v1

--- a/solution.py
+++ b/solution.py
@@ -54,10 +54,10 @@
 
 def kernel(
     n_sky, n_band,
-    img, mask, rk, ck, pr, pc, eg, zp,
+    img, mask, rk_in, ck_in, pr_in, pc_in, eg_in, zp_in,
     coadd_out, det_out,
-    x, msk, taps_r, taps_c, trow, wh, wl, vals, lists, other, cpad, energy, peer_energy, sums, det,
-    img_sem, mask_sem, halo_send, halo_recv, list_send, list_recv, co_send, co_recv, sum_send, sum_recv,
+    rk, ck, pr, pc, eg, zp, x, msk, taps_r, taps_c, trow, wh, wl, vals, lists, other, cpad, energy, peer_energy, sums, det,
+    arg_sem, img_sem, mask_sem, halo_send, halo_recv, list_send, list_recv, co_send, co_recv, sum_send, sum_recv,
     en_send, en_recv, out_sem,
 ):
     visits, height, columns = img.shape[1:]
@@ -68,6 +68,14 @@
     n_peer = n_sky * n_band
     me = sky * n_band + band
 
+    small = [
+        pltpu.make_async_copy(source, target, arg_sem.at[k])
+        for k, (source, target) in enumerate(
+            ((eg_in, eg), (zp_in, zp), (ck_in, ck), (pc_in, pc), (rk_in, rk), (pr_in, pr))
+        )
+    ]
+    for copy in small:
+        copy.start()
     load_img = pltpu.make_async_copy(img.at[0], x.at[:, pl.ds(PAD, height), :], img_sem)
     load_img.start()
     load_mask = pltpu.make_async_copy(mask.at[0], msk, mask_sem)
@@ -84,10 +92,13 @@
 
     taps_r[...] = jnp.zeros_like(taps_r)
     taps_c[...] = jnp.zeros_like(taps_c)
-    taps_r[0:visits, 0:TAPS] = rk[0]
+    for copy in small:
+        copy.wait()
+    for v in range(visits):
+        taps_r[v:v + 1, 0:TAPS] = rk[v]
     taps_r[visits:visits + 1, 0:TAPS] = pr[...]
     for v in range(visits):
-        taps_c[v:v + 1, 0:TAPS] = ck[0, v:v + 1] * zp[0, eg[0, v]]
+        taps_c[v:v + 1, 0:TAPS] = ck[v] * zp[0, eg[0, v]]
     taps_c[visits:visits + 1, 0:TAPS] = pc[...]
     at_row = lax.broadcasted_iota(jnp.int32, (TILE, TILE), 0)
     at_col = lax.broadcasted_iota(jnp.int32, (TILE, TILE), 1)
@@ -340,9 +351,7 @@
         crows = height // CHUNKS
         kernels = visits + 1
         table = -(-kernels // 8) * 8
-        vmem, smem, hbm = (
-            pl.BlockSpec(memory_space=space) for space in (pltpu.VMEM, pltpu.SMEM, pl.ANY)
-        )
+        hbm, anywhere = (pl.BlockSpec(memory_space=space) for space in (pltpu.HBM, pl.ANY))
         dma = pltpu.SemaphoreType.DMA
         return pl.pallas_call(
             functools.partial(kernel, n_sky, n_band),
@@ -350,9 +359,15 @@
                 jax.ShapeDtypeStruct((1, height, columns), F32),
                 jax.ShapeDtypeStruct((height, width), F32),
             ),
-            in_specs=[hbm, hbm, vmem, vmem, vmem, vmem, smem, smem],
-            out_specs=(hbm, hbm),
+            in_specs=[hbm] * 8,
+            out_specs=(anywhere, anywhere),
             scratch_shapes=[
+                pltpu.VMEM((visits, 1, TAPS), F32),
+                pltpu.VMEM((visits, 1, TAPS), F32),
+                pltpu.VMEM((1, TAPS), F32),
+                pltpu.VMEM((1, TAPS), F32),
+                pltpu.SMEM(exp_group.shape, jnp.int32),
+                pltpu.SMEM(zero_point.shape, F32),
                 pltpu.VMEM((visits, tall, columns), BF),
                 pltpu.VMEM((visits, height, columns), jnp.int32),
                 pltpu.VMEM((table, TILE), F32),
@@ -368,13 +383,13 @@
                 pltpu.VMEM((n_band - 1, height, width), F32),
                 pltpu.VMEM((n_sky * n_band, 8, TILE), F32),
                 pltpu.VMEM((height, width), F32),
-                dma, dma, dma((2, visits)), dma((2, visits)), dma((CHUNKS,)), dma((CHUNKS,)),
+                dma((6,)), dma, dma, dma((2, visits)), dma((2, visits)), dma((CHUNKS,)), dma((CHUNKS,)),
                 dma((2,)), dma((2,)), dma((n_sky * n_band - 1,)), dma((n_sky * n_band - 1,)), dma((n_band - 1,)), dma((n_band - 1,)), dma((2,)),
             ],
             compiler_params=pltpu.CompilerParams(
-                collective_id=0, has_side_effects=True, vmem_limit_bytes=48 * 1024 * 1024
+                collective_id=0, has_side_effects=True, vmem_limit_bytes=67043328
             ),
-        )(images, valid_mask, row_kernel, col_kernel, psf_row, psf_col, exp_group, zero_point)
+        )(images, valid_mask, jnp.swapaxes(row_kernel, 0, 1), jnp.swapaxes(col_kernel, 0, 1), psf_row, psf_col, exp_group, zero_point)
 
     placed = (
         P("band", "exp", ("patch", "sky"), None),

time: 37.4 us -> 32.2 us (0.86)
  local copies, waits for them, and re-layouts: 8.42 us -> 3.24 us
    unnamed x16 -> x2, local copies, waits for them, and re-layouts: 8.42 us -> 3.24 us
where the time goes in v2:
time: 32.2 us; the launch traced here: 32.1 us
  Pallas kernels  28.2 us (88%)
  local copies, waits for them, and re-layouts  3.24 us (10%)
  between operations  0.64 us (2%)
    pallas_call x1, Pallas kernels, on_device(): pl.pallas_call(functools.partial(kernel, n_sky, n_band), out_shape=(jax.S...  28.2 us
    unnamed x2, local copies, waits for them, and re-layouts  3.24 us

profile of v2, /device:TPU:0, one launch (start us, length us, event | category | flops | bytes accessed | tf_op | source)
XLA Modules:
  0.0 32.1 jit_solution(1454566322508859522)
XLA Ops:
  0.6 28.2 %shard_map.95 = (f32[1,128,512]{2,1,0:T(8,128)}, f32[128,256]{1,0:T(8,128)}) custom-call(bf16[1,10,128,512]{3,2,1,0:T(8,128)(2,1)} %img.1, s32[1,10,128,512]{3,2,1,0:T(8,128)} %mask.1, f32[10,1,31]{2,1,0:T(1,128)} %bitcast.2, f32[10,1,31]{2,1,0:T(1,128)} %bitcast.3, f32[1,31]{1,0:T(1,128)} %pr_in.1, f32[1,31]{1,0:T(1,128)} %pc_in.1, s32[1,10]{1,0:T(1,128)} %eg_in.1, ...), custom_call_target="tpu_custom_call" | custom-call | tf_op jit(solution)/shard_map/pallas_call | solution.py:356
  28.8 1.7 %copy.12 = f32[1,128,512]{2,1,0:T(8,128)} copy(f32[1,128,512]{2,1,0:T(8,128)} %get-tuple-element.4) | data formatting | bytes 524288
  30.5 1.6 %copy.13 = f32[128,256]{1,0:T(8,128)} copy(f32[128,256]{1,0:T(8,128)} %get-tuple-element.5) | data formatting | bytes 262144

commit v3 on v2

--- a/solution.py
+++ b/solution.py
@@ -57,7 +57,7 @@
     img, mask, rk_in, ck_in, pr_in, pc_in, eg_in, zp_in,
     coadd_out, det_out,
     rk, ck, pr, pc, eg, zp, x, msk, taps_r, taps_c, trow, wh, wl, vals, lists, other, cpad, energy, peer_energy, sums, det,
-    arg_sem, img_sem, mask_sem, halo_send, halo_recv, list_send, list_recv, co_send, co_recv, sum_send, sum_recv,
+    arg_sem, img_sem, mask_sem, halo_send, halo_recv, list_send, list_recv, share_send, share_recv, co_send, co_recv, sum_send, sum_recv,
     en_send, en_recv, out_sem,
 ):
     visits, height, columns = img.shape[1:]
@@ -128,7 +128,7 @@
                     ref[v, k * TILE:(k + 1) * TILE, n * TILE:(n + 1) * TILE] = block
         return carry
 
-    lax.fori_loop(0, visits + 1, build, 0)
+    lax.fori_loop(0, visits // 2, build, 0)
     pl.semaphore_wait(barrier, n_peer)
 
     def halo(v, side):
@@ -151,6 +151,7 @@
         return carry
 
     lax.fori_loop(0, visits, start_halo, 0)
+    lax.fori_loop(visits // 2, visits + 1, build, 0)
 
     @pl.when(jnp.logical_not(has_before))
     def _():
@@ -165,30 +166,42 @@
     load_img.wait()
     tall = height + 2 * PAD
 
-    def convolve(v, carry):
+    once = 2 - visits % 2
+
+    def convolve(i, carry):
         @pl.when(has_before)
         def _():
-            halo(v, 0).wait_recv()
+            for u in range(once):
+                halo(i * once + u, 0).wait_recv()
 
         @pl.when(has_after)
         def _():
-            halo(v, 1).wait_recv()
-        smeared = mm(trow[v, :, 0:tall], x[v])
-        high, low = parts(smeared[0:height] + smeared[height:])
-        for n, block in enumerate(cols_filter(high, low, wh.at[v], wl.at[v])):
-            vals[v, :, n * 2 * TILE:(n + 1) * 2 * TILE] = block
-        return carry
-
-    lax.fori_loop(0, visits, convolve, 0)
+            for u in range(once):
+                halo(i * once + u, 1).wait_recv()
+        smeared = [mm(trow[i * once + u, :, 0:tall], x[i * once + u]) for u in range(once)]
+        for u in range(once):
+            v = i * once + u
+            high, low = parts(smeared[u][0:height] + smeared[u][height:])
+            for n, block in enumerate(cols_filter(high, low, wh.at[v], wl.at[v])):
+                vals[v, :, n * 2 * TILE:(n + 1) * 2 * TILE] = block
+        return carry
+
+    lax.fori_loop(0, visits // once, convolve, 0)
     load_mask.wait()
 
+    half = CHUNKS // 2
+    own_first = exp * half
+    far_first = (1 - exp) * half
+
     def exchange(c):
         return pltpu.make_async_remote_copy(
-            src_ref=lists.at[c], dst_ref=other.at[c], send_sem=list_send.at[c], recv_sem=list_recv.at[c],
+            src_ref=lists.at[far_first + c], dst_ref=other.at[c], send_sem=list_send.at[c], recv_sem=list_recv.at[c],
             device_id={"exp": 1 - exp}, device_id_type=MESH,
         )
 
-    def select(c, carry):
+    def select(order, carry):
+        c = lax.rem(far_first + order, CHUNKS)
+
         def group(g, inner):
             rows = pl.ds(pl.multiple_of(c * crows + g * 8, 8), 8)
             upper, lower, total, count = [], [], None, None
@@ -206,18 +219,29 @@
             return inner
 
         lax.fori_loop(0, crows // 8, group, 0)
-        exchange(c).start()
+
+        @pl.when(order < half)
+        def _():
+            exchange(order).start()
         return carry
 
     lax.fori_loop(0, CHUNKS, select, 0)
 
-    def merge(c, carry):
-        exchange(c).wait_recv()
+    def share(first, j):
+        rows = pl.ds(pl.multiple_of(PAD + (first + j) * crows, 8), crows)
+        return pltpu.make_async_remote_copy(
+            src_ref=cpad.at[rows, :], dst_ref=cpad.at[rows, :], send_sem=share_send.at[j], recv_sem=share_recv.at[j],
+            device_id={"exp": 1 - exp}, device_id_type=MESH,
+        )
+
+    def merge(j, carry):
+        exchange(j).wait_recv()
+        c = own_first + j
 
         def group(g, inner):
             spot = pl.ds(pl.multiple_of(g * 8, 8), 8)
             own = [lists[c, k, spot, :] for k in range(2 * REJECT + 2)]
-            far = [other[c, k, spot, :] for k in range(2 * REJECT + 2)]
+            far = [other[j, k, spot, :] for k in range(2 * REJECT + 2)]
             ends = [jnp.maximum(own[k], far[REJECT - 1 - k]) for k in range(REJECT)]
             ends += [jnp.minimum(own[REJECT + k], far[2 * REJECT - 1 - k]) for k in range(REJECT)]
             upper_sum = (ends[0] + ends[1]) + (ends[2] + ends[3])
@@ -228,9 +252,12 @@
             return inner
 
         lax.fori_loop(0, crows // 8, group, 0)
-        return carry
-
-    lax.fori_loop(0, CHUNKS, merge, 0)
+        share(own_first, j).start()
+        return carry
+
+    lax.fori_loop(0, half, merge, 0)
+    for j in range(half):
+        share(far_first, j).wait_recv()
 
     def co_halo(side):
         start, land = ((height, 0), (PAD, PAD + height))[side]
@@ -329,8 +356,9 @@
     @pl.when(has_before)
     def _():
         co_halo(1).wait_send()
-    for c in range(CHUNKS):
-        exchange(c).wait_send()
+    for j in range(half):
+        exchange(j).wait_send()
+        share(own_first, j).wait_send()
     for step in range(1, n_peer):
         send_sum(step).wait_send()
     for step in range(1, n_band):
@@ -377,17 +405,17 @@
                 pltpu.VMEM((kernels, 4 * TILE, 2 * TILE), BF),
                 pltpu.VMEM((visits, height, columns), F32),
                 pltpu.VMEM((CHUNKS, n_list, crows, columns), F32),
-                pltpu.VMEM((CHUNKS, n_list, crows, columns), F32),
+                pltpu.VMEM((CHUNKS // 2, n_list, crows, columns), F32),
                 pltpu.VMEM((tall, columns), F32),
                 pltpu.VMEM((height, columns), F32),
                 pltpu.VMEM((n_band - 1, height, width), F32),
                 pltpu.VMEM((n_sky * n_band, 8, TILE), F32),
                 pltpu.VMEM((height, width), F32),
-                dma((6,)), dma, dma, dma((2, visits)), dma((2, visits)), dma((CHUNKS,)), dma((CHUNKS,)),
+                dma((6,)), dma, dma, dma((2, visits)), dma((2, visits)), dma((CHUNKS // 2,)), dma((CHUNKS // 2,)), dma((CHUNKS // 2,)), dma((CHUNKS // 2,)),
                 dma((2,)), dma((2,)), dma((n_sky * n_band - 1,)), dma((n_sky * n_band - 1,)), dma((n_band - 1,)), dma((n_band - 1,)), dma((2,)),
             ],
             compiler_params=pltpu.CompilerParams(
-                collective_id=0, has_side_effects=True, vmem_limit_bytes=67043328
+                collective_id=0, has_side_effects=True, vmem_limit_bytes=66600000
             ),
         )(images, valid_mask, jnp.swapaxes(row_kernel, 0, 1), jnp.swapaxes(col_kernel, 0, 1), psf_row, psf_col, exp_group, zero_point)
 

time: 32.2 us -> 30.4 us (0.944)
  Pallas kernels: 28.2 us -> 26.4 us
    pallas_call x1, Pallas kernels: 28.2 us -> 26.4 us  [on_device(): pl.pallas_call(functools.partial(kernel, n_sky, n_band), out_shape=(jax.S...]
where the time goes in v3:
time: 30.4 us; the launch traced here: 30.2 us
  Pallas kernels  26.4 us (87%)
  local copies, waits for them, and re-layouts  3.24 us (11%)
  between operations  0.64 us (2%)
    pallas_call x1, Pallas kernels, on_device(): pl.pallas_call(functools.partial(kernel, n_sky, n_band), out_shape=(jax.S...  26.4 us
    unnamed x2, local copies, waits for them, and re-layouts  3.24 us

profile of v3, /device:TPU:0, one launch (start us, length us, event | category | flops | bytes accessed | tf_op | source)
XLA Modules:
  0.0 30.2 jit_solution(17374278673957031911)
XLA Ops:
  0.6 26.4 %shard_map.95 = (f32[1,128,512]{2,1,0:T(8,128)}, f32[128,256]{1,0:T(8,128)}) custom-call(bf16[1,10,128,512]{3,2,1,0:T(8,128)(2,1)} %img.1, s32[1,10,128,512]{3,2,1,0:T(8,128)} %mask.1, f32[10,1,31]{2,1,0:T(1,128)} %bitcast.2, f32[10,1,31]{2,1,0:T(1,128)} %bitcast.3, f32[1,31]{1,0:T(1,128)} %pr_in.1, f32[1,31]{1,0:T(1,128)} %pc_in.1, s32[1,10]{1,0:T(1,128)} %eg_in.1, ...), custom_call_target="tpu_custom_call" | custom-call | tf_op jit(solution)/shard_map/pallas_call | solution.py:384
  27.0 1.7 %copy.12 = f32[1,128,512]{2,1,0:T(8,128)} copy(f32[1,128,512]{2,1,0:T(8,128)} %get-tuple-element.4) | data formatting | bytes 524288
  28.7 1.6 %copy.13 = f32[128,256]{1,0:T(8,128)} copy(f32[128,256]{1,0:T(8,128)} %get-tuple-element.5) | data formatting | bytes 262144

commit v4 on v3

--- a/solution.py
+++ b/solution.py
@@ -166,7 +166,7 @@
     load_img.wait()
     tall = height + 2 * PAD
 
-    once = 2 - visits % 2
+    once = next(u for u in (5, 2, 1) if visits % u == 0)
 
     def convolve(i, carry):
         @pl.when(has_before)

time: 30.4 us -> 30.6 us (level)
  no operation moved by 1% of the time
where the time goes in v4:
time: 30.6 us; the launch traced here: 30.4 us
  Pallas kernels  26.5 us (87%)
  local copies, waits for them, and re-layouts  3.24 us (11%)
  between operations  0.64 us (2%)
    pallas_call x1, Pallas kernels, on_device(): pl.pallas_call(functools.partial(kernel, n_sky, n_band), out_shape=(jax.S...  26.5 us
    unnamed x2, local copies, waits for them, and re-layouts  3.24 us

profile of v4, /device:TPU:0, one launch (start us, length us, event | category | flops | bytes accessed | tf_op | source)
XLA Modules:
  0.0 30.4 jit_solution(13988373335032652661)
XLA Ops:
  0.6 26.5 %shard_map.95 = (f32[1,128,512]{2,1,0:T(8,128)}, f32[128,256]{1,0:T(8,128)}) custom-call(bf16[1,10,128,512]{3,2,1,0:T(8,128)(2,1)} %img.1, s32[1,10,128,512]{3,2,1,0:T(8,128)} %mask.1, f32[10,1,31]{2,1,0:T(1,128)} %bitcast.2, f32[10,1,31]{2,1,0:T(1,128)} %bitcast.3, f32[1,31]{1,0:T(1,128)} %pr_in.1, f32[1,31]{1,0:T(1,128)} %pc_in.1, s32[1,10]{1,0:T(1,128)} %eg_in.1, ...), custom_call_target="tpu_custom_call" | custom-call | tf_op jit(solution)/shard_map/pallas_call | solution.py:384
  27.2 1.7 %copy.12 = f32[1,128,512]{2,1,0:T(8,128)} copy(f32[1,128,512]{2,1,0:T(8,128)} %get-tuple-element.4) | data formatting | bytes 524288
  28.8 1.6 %copy.13 = f32[128,256]{1,0:T(8,128)} copy(f32[128,256]{1,0:T(8,128)} %get-tuple-element.5) | data formatting | bytes 262144
